TPU v7x, 32 devices: a whole 2x2x4 slice. The times are simulated.
32 devices in a mesh: uly: 8 (over z, y), blk: 4 (over x, core).
Axes of the slice: x: 2, y: 2, z: 4, core: 2. Of those that a mesh axis runs over, the one named last changes fastest.
Arguments:
- queries: bfloat16 [2048, 2048], P(('blk', 'uly')), may hold values from -20 to 20
- keys: bfloat16 [2048, 2048], P(('blk', 'uly')), may hold values from -20 to 20
- values: bfloat16 [2048, 2048], P(('blk', 'uly')), may hold values from -6 to 6
- block_list: int32 [32, 16, 16], P('uly', 'blk'), may hold values from -1 to 15, as said below
Outputs:
- attended: bfloat16 [2048, 2048], P(('blk', 'uly'))
Inputs may be any that keep to these rules, and one draw needn't show every extreme that they name: block_list[h, b, 0] = b; every other entry is -1 (an empty slot) or a block below b, and the blocks named in one list are distinct.
All inputs are finite; a program needn't handle non-finite values.
Results may differ from a plain program's by a relative error of at most 0.0045.
Values may be sent and summed in bfloat16 or wider, within the bound.
No kernel may reach another device: no remote copies, remote signals or barrier semaphores. Data moves between devices by JAX's collectives and lax.ppermute only.
A program may use at most 64 MiB of HBM per device.

v0:
```python
import jax
import jax.numpy as jnp
from jax import lax
from jax.sharding import PartitionSpec as P

BLOCK = 128
QGROUP = 2


def head_major(token_rows, heads_local, head_dim):
    return token_rows.reshape(token_rows.shape[0] // BLOCK, BLOCK, heads_local, head_dim).transpose(
        2, 0, 1, 3
    )


def select_blocks(source, chosen):
    return jnp.take(source, chosen, axis=0)


def attend_block(operand):
    query_group, key_slots, value_slots, chosen, query_block = operand
    scale = query_group.shape[-1] ** (-0.5)
    scores = (
        jnp.einsum("abd,asjd->absj", query_group, key_slots, preferred_element_type=jnp.float32)
        * scale
    )
    positions = jnp.arange(BLOCK, dtype=jnp.int32)
    query_pos = query_block[:, None] * BLOCK + positions[None, :]
    key_pos = jnp.maximum(chosen, 0)[:, :, None] * BLOCK + positions[None, None, :]
    allowed = (chosen[:, None, :, None] >= 0) & (
        key_pos[:, None, :, :] <= query_pos[:, :, None, None]
    )
    scores = jnp.where(allowed, scores, -1e30)
    row_max = jnp.max(scores, axis=(2, 3), keepdims=True)
    weights = jnp.where(allowed, jnp.exp(scores - row_max), 0.0)
    denominator = jnp.sum(weights, axis=(2, 3))
    rounded = weights.astype(jnp.bfloat16)
    summed = jnp.einsum("absj,asjd->abd", rounded, value_slots, preferred_element_type=jnp.float32)
    return (summed / denominator[:, :, None]).astype(jnp.bfloat16)


def local(queries, keys, values, block_list):
    heads_local = block_list.shape[0]
    blocks_dev = block_list.shape[1]
    slot_count = block_list.shape[2]
    head_dim = queries.shape[1] // (heads_local * lax.axis_size("uly"))
    first_block = lax.axis_index("blk") * blocks_dev
    query_rows, key_rows, value_rows = (
        lax.all_to_all(queries, "uly", split_axis=1, concat_axis=0, tiled=True),
        lax.all_to_all(keys, "uly", split_axis=1, concat_axis=0, tiled=True),
        lax.all_to_all(values, "uly", split_axis=1, concat_axis=0, tiled=True),
    )
    keys_all = lax.all_gather(key_rows, "blk", axis=0, tiled=True)
    values_all = lax.all_gather(value_rows, "blk", axis=0, tiled=True)
    chosen = jnp.maximum(block_list, 0)
    key_slots = jax.vmap(select_blocks)(head_major(keys_all, heads_local, head_dim), chosen)
    value_slots = jax.vmap(select_blocks)(head_major(values_all, heads_local, head_dim), chosen)
    key_slots, value_slots = (key_slots, value_slots)
    groups = heads_local * blocks_dev // QGROUP
    query_heads = head_major(query_rows, heads_local, head_dim).reshape(
        groups, QGROUP, BLOCK, head_dim
    )
    key_groups = key_slots.reshape(groups, QGROUP, slot_count, BLOCK, head_dim)
    value_groups = value_slots.reshape(groups, QGROUP, slot_count, BLOCK, head_dim)
    list_groups = block_list.reshape(groups, QGROUP, slot_count)
    block_numbers = first_block + jnp.arange(blocks_dev, dtype=jnp.int32)
    block_groups = jnp.broadcast_to(block_numbers[None, :], (heads_local, blocks_dev)).reshape(
        groups, QGROUP
    )
    result = lax.map(
        attend_block, (query_heads, key_groups, value_groups, list_groups, block_groups)
    )
    result = result.reshape(heads_local, blocks_dev * BLOCK, head_dim).transpose(1, 0, 2)
    result = result.reshape(blocks_dev * BLOCK, heads_local * head_dim)
    return lax.all_to_all(result, "uly", split_axis=0, concat_axis=1, tiled=True)


def solution(mesh):
    placed = (
        P(("blk", "uly"), None),
        P(("blk", "uly"), None),
        P(("blk", "uly"), None),
        P("uly", "blk", None),
    )
    return jax.shard_map(
        local, mesh=mesh, in_specs=placed, out_specs=P(("blk", "uly"), None), check_vma=False
    )
```

profile of v0, /device:TPU:0, one launch (start us, length us, event | category | flops | bytes accessed | tf_op | source)
XLA Modules:
  0.0 148.7 jit_solution(14057702400680355051)
XLA Ops:
  7.6 16.1 %all_to_all.73 = bf16[64,8,256]{2,0,1:T(8,128)(2,1)} all-to-all(bf16[64,8,256]{2,0,1:T(8,128)(2,1)S(1)} %bitcast.102), channel_id=1, replica_groups=mesh['uly'=8,'blk'=4] {'uly'}, dimensions={1} | all-to-all | bytes 524288 | tf_op jit(solution)/shard_map/all_to_all | solution.py:50
  24.7 12.1 %all_to_all.74 = bf16[64,8,256]{2,0,1:T(8,128)(2,1)} all-to-all(bf16[64,8,256]{2,0,1:T(8,128)(2,1)S(1)} %bitcast.103), channel_id=1, replica_groups=mesh['uly'=8,'blk'=4] {'uly'}, dimensions={1} | all-to-all | bytes 524288 | tf_op jit(solution)/shard_map/all_to_all | solution.py:51
  37.5 3.6 %all-to-all-start = ((bf16[64,8,256]{2,0,1:T(8,128)(2,1)}), bf16[64,8,256]{2,0,1:T(8,128)(2,1)S(1)}, u32[]{:S(2)}, u32[]{:S(2)}) async-start(bf16[64,8,256]{2,0,1:T(8,128)(2,1)} %bitcast.73), calls=%async_computation | async-start | bytes 524288 | tf_op jit(solution)/shard_map/all_to_all | solution.py:49
  41.3 8.3 %all-to-all-done = bf16[64,8,256]{2,0,1:T(8,128)(2,1)S(1)} async-done(((bf16[64,8,256]{2,0,1:T(8,128)(2,1)}), bf16[64,8,256]{2,0,1:T(8,128)(2,1)S(1)}, u32[]{:S(2)}, u32[]{:S(2)}) %all-to-all-start) | async-done | bytes 262176 | tf_op jit(solution)/shard_map/all_to_all | solution.py:49
  50.3 3.3 %reshape.151 = bf16[16,128,4,64]{3,2,1,0:T(4,128)(2,1)S(1)} reshape(bf16[2048,256]{1,0:T(8,128)(2,1)} %all-gather.3.cloned.1.call-done) | data formatting | bytes 2097152 | tf_op jit(solution)/shard_map/reshape | solution.py:11
  55.0 2.8 %all-gather.5.cloned.1.call-done = bf16[2048,256]{1,0:T(8,128)(2,1)} async-done(((bf16[512,256]{1,0:T(8,128)(2,1)}), bf16[2048,256]{1,0:T(8,128)(2,1)}) %all-gather.5.cloned.1.call-update) | async-done | bytes 1048592 | tf_op jit(solution)/shard_map/all_gather | solution.py:54
  57.9 4.4 %reshape.152 = bf16[16,128,4,64]{3,2,1,0:T(4,128)(2,1)} reshape(bf16[2048,256]{1,0:T(8,128)(2,1)} %all-gather.5.cloned.1.call-done) | data formatting | bytes 2097152 | tf_op jit(solution)/shard_map/reshape | solution.py:11
  62.3 3.0 %copy.52 = bf16[16,128,4,64]{1,3,0,2:T(8,128)(2,1)S(1)} copy(bf16[16,128,4,64]{3,2,1,0:T(4,128)(2,1)} %reshape.152) | data formatting | bytes 2097152 | tf_op jit(solution)/shard_map/reshape | solution.py:11
  65.3 3.3 %gather_fusion = bf16[256,128,64]{1,2,0:T(8,128)(2,1)} fusion(bf16[4,16,128,64]{2,3,1,0:T(8,128)(2,1)S(1)} %bitcast.90, s32[256]{0:T(256)S(1)} %reshape.139), kind=kCustom, calls=%fused_computation.clone | custom fusion | bytes 8390656 | tf_op jit(solution)/shard_map/vmap(jit(_take))/gather | solution.py:17
  68.6 3.3 %gather_fusion.1 = bf16[256,128,64]{1,2,0:T(8,128)(2,1)} fusion(bf16[4,16,128,64]{2,3,1,0:T(8,128)(2,1)S(1)} %bitcast.91, s32[256]{0:T(256)S(1)} %reshape.139), kind=kCustom, calls=%fused_computation.1.clone | custom fusion | bytes 8390656 | tf_op jit(solution)/shard_map/vmap(jit(_take))/gather | solution.py:17
  72.0 5.9 %broadcast_select_fusion = (bf16[4,4,16,128,64]{3,4,2,1,0:T(8,128)(2,1)}, bf16[4,4,16,128,64]{3,4,2,1,0:T(8,128)(2,1)}) fusion(bf16[4,4,16,128,64]{3,4,2,1,0:T(8,128)(2,1)} %bitcast.93, pred[4,4,16]{2,1,0:T(4,128)(4,1)S(1)} %maximum_compare_fusion, bf16[4,4,16,128,64]{3,4,2,1,0:T(8,128)(2,1)} %bitcast.92), kind=kLoop, calls=%fused_computation.33 | loop fusion | flops 4194304 | bytes 16777472 | tf_op jit(solution)/shard_map/vmap(jit(_take))/select_n | solution.py:17
  77.9 47.7 %while.10 = (s32[]{:T(128)}, bf16[8,2,128,64]{2,1,0,3:T(2,128)(2,1)S(1)}, s32[8,2,16]{2,1,0:T(2,128)S(1)}, s32[8,2]{1,0:T(8,128)S(1)}, bf16[8,2,128,64]{2,3,1,0:...) while((s32[]{:T(128)}, ...), condition=%wide.region_3.5_spmd, body=%wide.region_0.4_spmd.sunk | while | flops 142118752 | bytes 7548637 | solution.py:70
  78.1 2.9 %fusion.31 = (f32[2,128]{1,0:T(2,128)S(1)}, f32[2,128,16,128]{1,3,2,0:T(8,128)S(1)}) fusion(bf16[8,2,16,128,64]{3,4,2,1,0:T(8,128)(2,1)} %get-tuple-element.165, s32[]{:T(128)} %get-tuple-element.152, bf16[8,2,128,64]{2,3,1,0:T(8,128)(2,1)S(1)} %get-tuple-element.164, s32[2,128]{1,0:T(2,128)S(1)} %iota_add_fusion.4, ...), kind=kOutput, calls=%fused_computation.41.clone.1 | convolution fusion | flops 69730048 | bytes 2674176 | tf_op jit(solution)/shard_map/while/body/eval_jaxpr/abd,asjd->absj/dot_general | solution.py:24
  81.8 2.1 %fusion.33 = bf16[1,2,128,64]{2,3,1,0:T(8,128)(2,1)S(1)} fusion(f32[2,128,16,128]{1,3,2,0:T(8,128)S(1)} %get-tuple-element.142, f32[2,128]{1,0:T(2,128)S(1)} %get-tuple-element.143, s32[2,128]{1,0:T(2,128)S(1)} %iota_add_fusion.4, s32[2,16,128]{2,1,0:T(8,128)S(1)} %iota_add_fusion.5, pred[2,16]{1,0:T(4,128)(4,1)S(1)} %compare_bitcast_fusion.2, ...), kind=kOutput, calls=%fused_computation.10.clone.1 | convolution fusion | flops 69763072 | bytes 2674208 | tf_op jit(solution)/shard_map/while/body/eval_jaxpr/absj,asjd->abd/dot_general | solution.py:38
  84.1 2.9 %fusion.31 = (f32[2,128]{1,0:T(2,128)S(1)}, f32[2,128,16,128]{1,3,2,0:T(8,128)S(1)}) fusion(bf16[8,2,16,128,64]{3,4,2,1,0:T(8,128)(2,1)} %get-tuple-element.165, s32[]{:T(128)} %get-tuple-element.152, bf16[8,2,128,64]{2,3,1,0:T(8,128)(2,1)S(1)} %get-tuple-element.164, s32[2,128]{1,0:T(2,128)S(1)} %iota_add_fusion.4, ...), kind=kOutput, calls=%fused_computation.41.clone.1 | convolution fusion | flops 69730048 | bytes 2674176 | tf_op jit(solution)/shard_map/while/body/eval_jaxpr/abd,asjd->absj/dot_general | solution.py:24
  90.1 2.9 %fusion.31 = (f32[2,128]{1,0:T(2,128)S(1)}, f32[2,128,16,128]{1,3,2,0:T(8,128)S(1)}) fusion(bf16[8,2,16,128,64]{3,4,2,1,0:T(8,128)(2,1)} %get-tuple-element.165, s32[]{:T(128)} %get-tuple-element.152, bf16[8,2,128,64]{2,3,1,0:T(8,128)(2,1)S(1)} %get-tuple-element.164, s32[2,128]{1,0:T(2,128)S(1)} %iota_add_fusion.4, ...), kind=kOutput, calls=%fused_computation.41.clone.1 | convolution fusion | flops 69730048 | bytes 2674176 | tf_op jit(solution)/shard_map/while/body/eval_jaxpr/abd,asjd->absj/dot_general | solution.py:24
  96.0 2.9 %fusion.31 = (f32[2,128]{1,0:T(2,128)S(1)}, f32[2,128,16,128]{1,3,2,0:T(8,128)S(1)}) fusion(bf16[8,2,16,128,64]{3,4,2,1,0:T(8,128)(2,1)} %get-tuple-element.165, s32[]{:T(128)} %get-tuple-element.152, bf16[8,2,128,64]{2,3,1,0:T(8,128)(2,1)S(1)} %get-tuple-element.164, s32[2,128]{1,0:T(2,128)S(1)} %iota_add_fusion.4, ...), kind=kOutput, calls=%fused_computation.41.clone.1 | convolution fusion | flops 69730048 | bytes 2674176 | tf_op jit(solution)/shard_map/while/body/eval_jaxpr/abd,asjd->absj/dot_general | solution.py:24
  99.7 2.1 %fusion.33 = bf16[1,2,128,64]{2,3,1,0:T(8,128)(2,1)S(1)} fusion(f32[2,128,16,128]{1,3,2,0:T(8,128)S(1)} %get-tuple-element.142, f32[2,128]{1,0:T(2,128)S(1)} %get-tuple-element.143, s32[2,128]{1,0:T(2,128)S(1)} %iota_add_fusion.4, s32[2,16,128]{2,1,0:T(8,128)S(1)} %iota_add_fusion.5, pred[2,16]{1,0:T(4,128)(4,1)S(1)} %compare_bitcast_fusion.2, ...), kind=kOutput, calls=%fused_computation.10.clone.1 | convolution fusion | flops 69763072 | bytes 2674208 | tf_op jit(solution)/shard_map/while/body/eval_jaxpr/absj,asjd->abd/dot_general | solution.py:38
  102.0 2.9 %fusion.31 = (f32[2,128]{1,0:T(2,128)S(1)}, f32[2,128,16,128]{1,3,2,0:T(8,128)S(1)}) fusion(bf16[8,2,16,128,64]{3,4,2,1,0:T(8,128)(2,1)} %get-tuple-element.165, s32[]{:T(128)} %get-tuple-element.152, bf16[8,2,128,64]{2,3,1,0:T(8,128)(2,1)S(1)} %get-tuple-element.164, s32[2,128]{1,0:T(2,128)S(1)} %iota_add_fusion.4, ...), kind=kOutput, calls=%fused_computation.41.clone.1 | convolution fusion | flops 69730048 | bytes 2674176 | tf_op jit(solution)/shard_map/while/body/eval_jaxpr/abd,asjd->absj/dot_general | solution.py:24
  108.0 2.9 %fusion.31 = (f32[2,128]{1,0:T(2,128)S(1)}, f32[2,128,16,128]{1,3,2,0:T(8,128)S(1)}) fusion(bf16[8,2,16,128,64]{3,4,2,1,0:T(8,128)(2,1)} %get-tuple-element.165, s32[]{:T(128)} %get-tuple-element.152, bf16[8,2,128,64]{2,3,1,0:T(8,128)(2,1)S(1)} %get-tuple-element.164, s32[2,128]{1,0:T(2,128)S(1)} %iota_add_fusion.4, ...), kind=kOutput, calls=%fused_computation.41.clone.1 | convolution fusion | flops 69730048 | bytes 2674176 | tf_op jit(solution)/shard_map/while/body/eval_jaxpr/abd,asjd->absj/dot_general | solution.py:24
  113.9 2.9 %fusion.31 = (f32[2,128]{1,0:T(2,128)S(1)}, f32[2,128,16,128]{1,3,2,0:T(8,128)S(1)}) fusion(bf16[8,2,16,128,64]{3,4,2,1,0:T(8,128)(2,1)} %get-tuple-element.165, s32[]{:T(128)} %get-tuple-element.152, bf16[8,2,128,64]{2,3,1,0:T(8,128)(2,1)S(1)} %get-tuple-element.164, s32[2,128]{1,0:T(2,128)S(1)} %iota_add_fusion.4, ...), kind=kOutput, calls=%fused_computation.41.clone.1 | convolution fusion | flops 69730048 | bytes 2674176 | tf_op jit(solution)/shard_map/while/body/eval_jaxpr/abd,asjd->absj/dot_general | solution.py:24
  117.6 2.1 %fusion.33 = bf16[1,2,128,64]{2,3,1,0:T(8,128)(2,1)S(1)} fusion(f32[2,128,16,128]{1,3,2,0:T(8,128)S(1)} %get-tuple-element.142, f32[2,128]{1,0:T(2,128)S(1)} %get-tuple-element.143, s32[2,128]{1,0:T(2,128)S(1)} %iota_add_fusion.4, s32[2,16,128]{2,1,0:T(8,128)S(1)} %iota_add_fusion.5, pred[2,16]{1,0:T(4,128)(4,1)S(1)} %compare_bitcast_fusion.2, ...), kind=kOutput, calls=%fused_computation.10.clone.1 | convolution fusion | flops 69763072 | bytes 2674208 | tf_op jit(solution)/shard_map/while/body/eval_jaxpr/absj,asjd->abd/dot_general | solution.py:38
  119.9 2.9 %fusion.31 = (f32[2,128]{1,0:T(2,128)S(1)}, f32[2,128,16,128]{1,3,2,0:T(8,128)S(1)}) fusion(bf16[8,2,16,128,64]{3,4,2,1,0:T(8,128)(2,1)} %get-tuple-element.165, s32[]{:T(128)} %get-tuple-element.152, bf16[8,2,128,64]{2,3,1,0:T(8,128)(2,1)S(1)} %get-tuple-element.164, s32[2,128]{1,0:T(2,128)S(1)} %iota_add_fusion.4, ...), kind=kOutput, calls=%fused_computation.41.clone.1 | convolution fusion | flops 69730048 | bytes 2674176 | tf_op jit(solution)/shard_map/while/body/eval_jaxpr/abd,asjd->absj/dot_general | solution.py:24
  126.5 14.6 %all_to_all.75 = bf16[8,64,256]{2,1,0:T(8,128)(2,1)S(1)} all-to-all(bf16[8,64,256]{2,1,0:T(8,128)(2,1)S(1)} %reshape.153), channel_id=1, replica_groups=mesh['uly'=8,'blk'=4] {'uly'}, dimensions={0} | all-to-all | bytes 524288 | tf_op jit(solution)/shard_map/all_to_all | solution.py:75
  (89 shorter events, 24.8 us)
Async XLA Ops:
  6.5 30.3 %copy-start = (bf16[64,2048]{1,0:T(8,128)(2,1)S(1)}, bf16[64,2048]{1,0:T(8,128)(2,1)}, u32[]{:S(2)}) copy-start(bf16[64,2048]{1,0:T(8,128)(2,1)} %param.8) | copy-start | bytes 786436
  6.5 34.6 %copy-start.2 = (s32[4,4,16]{2,1,0:T(4,128)S(1)}, s32[4,4,16]{2,1,0:T(4,128)}, u32[]{:S(2)}) copy-start(s32[4,4,16]{2,1,0:T(4,128)} %param.11) | copy-start | bytes 3076
  6.5 43.7 %all-gather.3.cloned.1.call-start = ((), (), s32[]{:S(2)}) async-start(), calls=%async_computation.4 | async-start | bytes 1310720 | tf_op jit(solution)/shard_map/all_gather | solution.py:53
  23.7 34.1 %all-gather.5.cloned.1.call-start = ((), (), s32[]{:S(2)}) async-start(), calls=%async_computation.5 | async-start | bytes 1310720 | tf_op jit(solution)/shard_map/all_gather | solution.py:54
  37.5 12.1 %all-to-all-start = ((bf16[64,8,256]{2,0,1:T(8,128)(2,1)}), bf16[64,8,256]{2,0,1:T(8,128)(2,1)S(1)}, u32[]{:S(2)}, u32[]{:S(2)}) async-start(bf16[64,8,256]{2,0,1:T(8,128)(2,1)} %bitcast.73), calls=%async_computation | async-start | bytes 524288 | tf_op jit(solution)/shard_map/all_to_all | solution.py:49
  72.0 6.0 %copy-start.1 = (bf16[8,2,128,64]{2,1,0,3:T(2,128)(2,1)S(1)}, bf16[8,2,128,64]{2,1,0,3:T(2,128)(2,1)}, u32[]{:S(2)}) copy-start(bf16[8,2,128,64]{2,1,0,3:T(2,128)(2,1)} %custom-call.6) | copy-start | bytes 786436
Sparse Core Ops, SparseCore 0:
  23.8 15.6 all-gather.2
  41.1 16.6 all-gather.4
where the time goes:
time: 150 us; the launch traced here: 149 us
  blocking collectives  42.8 us (29%)
  matrix products  39.3 us (26%)
  local copies, waits for them, and re-layouts  24.3 us (16%)
  other arithmetic  13.5 us (9%)
  between operations  13.5 us (9%)
  waiting for transfers between devices  11.2 us (7%)
  starting transfers between devices  3.63 us (2%)
    dot_general x8, matrix products, attend_block(): jnp.einsum('abd,asjd->absj', query_group, key_slots, preferred_element_ty...  22.8 us
    dot_general x8, matrix products, attend_block(): jnp.einsum('absj,asjd->abd', rounded, value_slots, preferred_element_type...  16.4 us
    all_to_all x1, blocking collectives, local(): lax.all_to_all(keys, 'uly', split_axis=1, concat_axis=0, tiled=True)  16.1 us
    all_to_all x1, blocking collectives, local(): lax.all_to_all(result, 'uly', split_axis=0, concat_axis=1, tiled=True)  14.6 us
    reshape x5, local copies, waits for them, and re-layouts, head_major(): token_rows.reshape(token_rows.shape[0] // BLOCK, BLOCK, heads_local, head...  12.4 us
    all_to_all x1, blocking collectives, local(): lax.all_to_all(values, 'uly', split_axis=1, concat_axis=0, tiled=True)  12.1 us
    all_to_all x1, waiting for transfers between devices, local(): lax.all_to_all(queries, 'uly', split_axis=1, concat_axis=0, tiled=True)  8.31 us
    gather x3, local copies, waits for them, and re-layouts, select_blocks(): return jnp.take(source, chosen, axis=0)  6.75 us
  transfers between devices with their start and end apart: 3, of which 2 were waited for; matrix products, arithmetic and copies ran while one was open for 5% of the time, Pallas kernels for 0%

commit v1 on v0

--- a/solution.py
+++ b/solution.py
@@ -48,7 +48,10 @@
     query_rows, key_rows, value_rows = (
         lax.all_to_all(queries, "uly", split_axis=1, concat_axis=0, tiled=True),
         lax.all_to_all(keys, "uly", split_axis=1, concat_axis=0, tiled=True),
-        lax.all_to_all(values, "uly", split_axis=1, concat_axis=0, tiled=True),
+        jnp.concatenate(
+            lax.all_to_all(jnp.stack(jnp.split(values, lax.axis_size("uly"), axis=1)), "uly", 0, 0),
+            axis=0,
+        ),
     )
     keys_all = lax.all_gather(key_rows, "blk", axis=0, tiled=True)
     values_all = lax.all_gather(value_rows, "blk", axis=0, tiled=True)

time: 150 us -> 156 us (1.040)
  local copies, waits for them, and re-layouts: 24.3 us -> 27.3 us
  waiting for transfers between devices: 11.2 us -> 14.2 us
    unnamed x7 -> x13, local copies, waits for them, and re-layouts: 0.11 us -> 6.92 us
    all_gather x1, waiting for transfers between devices: 0.02 us -> 5.83 us  [local(): keys_all = lax.all_gather(key_rows, 'blk', axis=0, tiled=True)]
    reshape x5 -> x4, local copies, waits for them, and re-layouts: 12.4 us -> 7.97 us  [head_major(): token_rows.reshape(token_rows.shape[0] // BLOCK, BLOCK, heads_local, head...]
    all_to_all x1, blocking collectives: 16.1 us -> 12.1 us  [local(): lax.all_to_all(keys, 'uly', split_axis=1, concat_axis=0, tiled=True)]
    all_to_all x1, blocking collectives: 12.1 us -> 16 us  [local(): lax.all_to_all(jnp.stack(jnp.split(values, lax.axis_size('uly'), axis=1))...]
    all_gather x1, waiting for transfers between devices: 2.84 us -> 0.02 us  [local(): values_all = lax.all_gather(value_rows, 'blk', axis=0, tiled=True)]
  transfers between devices with their start and end apart: 3 -> 3, of which waited for: 2 -> 2; matrix products, arithmetic and copies ran while one was open for 5% -> 3% of each run, Pallas kernels for 0% -> 0%
where the time goes in v1:
time: 156 us; the launch traced here: 154 us
  blocking collectives  42.7 us (27%)
  matrix products  39.3 us (25%)
  local copies, waits for them, and re-layouts  27.3 us (18%)
  waiting for transfers between devices  14.2 us (9%)
  other arithmetic  13.5 us (9%)
  between operations  13.5 us (9%)
  starting transfers between devices  3.63 us (2%)
    dot_general x8, matrix products, attend_block(): jnp.einsum('abd,asjd->absj', query_group, key_slots, preferred_element_ty...  22.8 us
    dot_general x8, matrix products, attend_block(): jnp.einsum('absj,asjd->abd', rounded, value_slots, preferred_element_type...  16.4 us
    all_to_all x1, blocking collectives, local(): lax.all_to_all(jnp.stack(jnp.split(values, lax.axis_size('uly'), axis=1))...  16 us
    all_to_all x1, blocking collectives, local(): lax.all_to_all(result, 'uly', split_axis=0, concat_axis=1, tiled=True)  14.6 us
    all_to_all x1, blocking collectives, local(): lax.all_to_all(keys, 'uly', split_axis=1, concat_axis=0, tiled=True)  12.1 us
    all_to_all x1, waiting for transfers between devices, local(): lax.all_to_all(queries, 'uly', split_axis=1, concat_axis=0, tiled=True)  8.31 us
    reshape x4, local copies, waits for them, and re-layouts, head_major(): token_rows.reshape(token_rows.shape[0] // BLOCK, BLOCK, heads_local, head...  7.97 us
    unnamed x13, local copies, waits for them, and re-layouts  6.92 us
  transfers between devices with their start and end apart: 3, of which 2 were waited for; matrix products, arithmetic and copies ran while one was open for 3% of the time, Pallas kernels for 0%

profile of v1, /device:TPU:0, one launch (start us, length us, event | category | flops | bytes accessed | tf_op | source)
XLA Modules:
  0.0 154.5 jit_solution(1320054926217198151)
XLA Ops:
  12.7 16.0 %all_to_all.59 = bf16[8,64,256]{2,1,0:T(8,128)(2,1)S(1)} all-to-all(bf16[8,64,256]{2,1,0:T(8,128)(2,1)S(1)} %bitcast_dynamic-update-slice_fusion), channel_id=1, replica_groups=mesh['uly'=8,'blk'=4] {'uly'}, dimensions={0} | all-to-all | bytes 524288 | tf_op jit(solution)/shard_map/all_to_all | solution.py:52
  30.6 12.1 %all_to_all.60 = bf16[64,8,256]{2,0,1:T(8,128)(2,1)} all-to-all(bf16[64,8,256]{2,0,1:T(8,128)(2,1)S(1)} %bitcast.121), channel_id=1, replica_groups=mesh['uly'=8,'blk'=4] {'uly'}, dimensions={1} | all-to-all | bytes 524288 | tf_op jit(solution)/shard_map/all_to_all | solution.py:50
  43.4 3.6 %all-to-all-start = ((bf16[64,8,256]{2,0,1:T(8,128)(2,1)}), bf16[64,8,256]{2,0,1:T(8,128)(2,1)S(1)}, u32[]{:S(2)}, u32[]{:S(2)}) async-start(bf16[64,8,256]{2,0,1:T(8,128)(2,1)} %bitcast.90), calls=%async_computation | async-start | bytes 524288 | tf_op jit(solution)/shard_map/all_to_all | solution.py:49
  47.2 8.3 %all-to-all-done = bf16[64,8,256]{2,0,1:T(8,128)(2,1)S(1)} async-done(((bf16[64,8,256]{2,0,1:T(8,128)(2,1)}), bf16[64,8,256]{2,0,1:T(8,128)(2,1)S(1)}, u32[]{:S(2)}, u32[]{:S(2)}) %all-to-all-start) | async-done | bytes 262176 | tf_op jit(solution)/shard_map/all_to_all | solution.py:49
  57.9 5.8 %all-gather.3.cloned.1.call-done = bf16[2048,256]{1,0:T(8,128)(2,1)} async-done(((bf16[512,256]{1,0:T(8,128)(2,1)}), bf16[2048,256]{1,0:T(8,128)(2,1)}) %all-gather.3.cloned.1.call-update) | async-done | bytes 1048592 | tf_op jit(solution)/shard_map/all_gather | solution.py:56
  63.7 4.4 %reshape.152 = bf16[16,128,4,64]{3,2,1,0:T(4,128)(2,1)} reshape(bf16[2048,256]{1,0:T(8,128)(2,1)} %all-gather.3.cloned.1.call-done) | data formatting | bytes 2097152 | tf_op jit(solution)/shard_map/reshape | solution.py:11
  68.1 3.0 %copy.47 = bf16[16,128,4,64]{1,3,0,2:T(8,128)(2,1)S(1)} copy(bf16[16,128,4,64]{3,2,1,0:T(4,128)(2,1)} %reshape.152) | data formatting | bytes 2097152 | tf_op jit(solution)/shard_map/reshape | solution.py:11
  71.2 3.4 %gather_fusion.1 = bf16[256,128,64]{1,2,0:T(8,128)(2,1)} fusion(bf16[4,16,128,64]{2,3,1,0:T(8,128)(2,1)S(1)} %bitcast.107, s32[256]{0:T(256)S(1)} %reshape.140), kind=kCustom, calls=%fused_computation.1.clone | custom fusion | bytes 8390656 | tf_op jit(solution)/shard_map/vmap(jit(_take))/gather | solution.py:17
  74.5 3.3 %gather_fusion = bf16[256,128,64]{1,2,0:T(8,128)(2,1)} fusion(bf16[4,16,128,64]{2,3,1,0:T(8,128)(2,1)S(1)} %bitcast.108, s32[256]{0:T(256)S(1)} %reshape.140), kind=kCustom, calls=%fused_computation.clone | custom fusion | bytes 8390656 | tf_op jit(solution)/shard_map/vmap(jit(_take))/gather | solution.py:17
  77.8 5.9 %broadcast_select_fusion = (bf16[4,4,16,128,64]{3,4,2,1,0:T(8,128)(2,1)}, bf16[4,4,16,128,64]{3,4,2,1,0:T(8,128)(2,1)}) fusion(bf16[4,4,16,128,64]{3,4,2,1,0:T(8,128)(2,1)} %bitcast.109, pred[4,4,16]{2,1,0:T(4,128)(4,1)S(1)} %maximum_compare_fusion, bf16[4,4,16,128,64]{3,4,2,1,0:T(8,128)(2,1)} %bitcast.110), kind=kLoop, calls=%fused_computation.33 | loop fusion | flops 4194304 | bytes 16777472 | tf_op jit(solution)/shard_map/vmap(jit(_take))/select_n | solution.py:17
  83.7 47.7 %while.10 = (s32[]{:T(128)}, bf16[8,2,128,64]{2,1,0,3:T(2,128)(2,1)S(1)}, s32[8,2,16]{2,1,0:T(2,128)S(1)}, s32[8,2]{1,0:T(8,128)S(1)}, bf16[8,2,128,64]{2,3,1,0:...) while((s32[]{:T(128)}, ...), condition=%wide.region_3.5_spmd, body=%wide.region_0.4_spmd.sunk | while | flops 142118752 | bytes 7548637 | solution.py:73
  83.9 2.9 %fusion.31 = (f32[2,128]{1,0:T(2,128)S(1)}, f32[2,128,16,128]{1,3,2,0:T(8,128)S(1)}) fusion(bf16[8,2,16,128,64]{3,4,2,1,0:T(8,128)(2,1)} %get-tuple-element.165, s32[]{:T(128)} %get-tuple-element.152, bf16[8,2,128,64]{2,3,1,0:T(8,128)(2,1)S(1)} %get-tuple-element.164, s32[2,128]{1,0:T(2,128)S(1)} %iota_add_fusion.4, ...), kind=kOutput, calls=%fused_computation.49.clone.1 | convolution fusion | flops 69730048 | bytes 2674176 | tf_op jit(solution)/shard_map/while/body/eval_jaxpr/abd,asjd->absj/dot_general | solution.py:24
  87.6 2.1 %fusion.33 = bf16[1,2,128,64]{2,3,1,0:T(8,128)(2,1)S(1)} fusion(f32[2,128,16,128]{1,3,2,0:T(8,128)S(1)} %get-tuple-element.142, f32[2,128]{1,0:T(2,128)S(1)} %get-tuple-element.143, s32[2,128]{1,0:T(2,128)S(1)} %iota_add_fusion.4, s32[2,16,128]{2,1,0:T(8,128)S(1)} %iota_add_fusion.5, pred[2,16]{1,0:T(4,128)(4,1)S(1)} %compare_bitcast_fusion.2, ...), kind=kOutput, calls=%fused_computation.10.clone.1 | convolution fusion | flops 69763072 | bytes 2674208 | tf_op jit(solution)/shard_map/while/body/eval_jaxpr/absj,asjd->abd/dot_general | solution.py:38
  89.9 2.9 %fusion.31 = (f32[2,128]{1,0:T(2,128)S(1)}, f32[2,128,16,128]{1,3,2,0:T(8,128)S(1)}) fusion(bf16[8,2,16,128,64]{3,4,2,1,0:T(8,128)(2,1)} %get-tuple-element.165, s32[]{:T(128)} %get-tuple-element.152, bf16[8,2,128,64]{2,3,1,0:T(8,128)(2,1)S(1)} %get-tuple-element.164, s32[2,128]{1,0:T(2,128)S(1)} %iota_add_fusion.4, ...), kind=kOutput, calls=%fused_computation.49.clone.1 | convolution fusion | flops 69730048 | bytes 2674176 | tf_op jit(solution)/shard_map/while/body/eval_jaxpr/abd,asjd->absj/dot_general | solution.py:24
  93.5 2.1 %fusion.33 = bf16[1,2,128,64]{2,3,1,0:T(8,128)(2,1)S(1)} fusion(f32[2,128,16,128]{1,3,2,0:T(8,128)S(1)} %get-tuple-element.142, f32[2,128]{1,0:T(2,128)S(1)} %get-tuple-element.143, s32[2,128]{1,0:T(2,128)S(1)} %iota_add_fusion.4, s32[2,16,128]{2,1,0:T(8,128)S(1)} %iota_add_fusion.5, pred[2,16]{1,0:T(4,128)(4,1)S(1)} %compare_bitcast_fusion.2, ...), kind=kOutput, calls=%fused_computation.10.clone.1 | convolution fusion | flops 69763072 | bytes 2674208 | tf_op jit(solution)/shard_map/while/body/eval_jaxpr/absj,asjd->abd/dot_general | solution.py:38
  95.8 2.9 %fusion.31 = (f32[2,128]{1,0:T(2,128)S(1)}, f32[2,128,16,128]{1,3,2,0:T(8,128)S(1)}) fusion(bf16[8,2,16,128,64]{3,4,2,1,0:T(8,128)(2,1)} %get-tuple-element.165, s32[]{:T(128)} %get-tuple-element.152, bf16[8,2,128,64]{2,3,1,0:T(8,128)(2,1)S(1)} %get-tuple-element.164, s32[2,128]{1,0:T(2,128)S(1)} %iota_add_fusion.4, ...), kind=kOutput, calls=%fused_computation.49.clone.1 | convolution fusion | flops 69730048 | bytes 2674176 | tf_op jit(solution)/shard_map/while/body/eval_jaxpr/abd,asjd->absj/dot_general | solution.py:24
  101.8 2.9 %fusion.31 = (f32[2,128]{1,0:T(2,128)S(1)}, f32[2,128,16,128]{1,3,2,0:T(8,128)S(1)}) fusion(bf16[8,2,16,128,64]{3,4,2,1,0:T(8,128)(2,1)} %get-tuple-element.165, s32[]{:T(128)} %get-tuple-element.152, bf16[8,2,128,64]{2,3,1,0:T(8,128)(2,1)S(1)} %get-tuple-element.164, s32[2,128]{1,0:T(2,128)S(1)} %iota_add_fusion.4, ...), kind=kOutput, calls=%fused_computation.49.clone.1 | convolution fusion | flops 69730048 | bytes 2674176 | tf_op jit(solution)/shard_map/while/body/eval_jaxpr/abd,asjd->absj/dot_general | solution.py:24
  107.8 2.9 %fusion.31 = (f32[2,128]{1,0:T(2,128)S(1)}, f32[2,128,16,128]{1,3,2,0:T(8,128)S(1)}) fusion(bf16[8,2,16,128,64]{3,4,2,1,0:T(8,128)(2,1)} %get-tuple-element.165, s32[]{:T(128)} %get-tuple-element.152, bf16[8,2,128,64]{2,3,1,0:T(8,128)(2,1)S(1)} %get-tuple-element.164, s32[2,128]{1,0:T(2,128)S(1)} %iota_add_fusion.4, ...), kind=kOutput, calls=%fused_computation.49.clone.1 | convolution fusion | flops 69730048 | bytes 2674176 | tf_op jit(solution)/shard_map/while/body/eval_jaxpr/abd,asjd->absj/dot_general | solution.py:24
  111.4 2.1 %fusion.33 = bf16[1,2,128,64]{2,3,1,0:T(8,128)(2,1)S(1)} fusion(f32[2,128,16,128]{1,3,2,0:T(8,128)S(1)} %get-tuple-element.142, f32[2,128]{1,0:T(2,128)S(1)} %get-tuple-element.143, s32[2,128]{1,0:T(2,128)S(1)} %iota_add_fusion.4, s32[2,16,128]{2,1,0:T(8,128)S(1)} %iota_add_fusion.5, pred[2,16]{1,0:T(4,128)(4,1)S(1)} %compare_bitcast_fusion.2, ...), kind=kOutput, calls=%fused_computation.10.clone.1 | convolution fusion | flops 69763072 | bytes 2674208 | tf_op jit(solution)/shard_map/while/body/eval_jaxpr/absj,asjd->abd/dot_general | solution.py:38
  113.7 2.9 %fusion.31 = (f32[2,128]{1,0:T(2,128)S(1)}, f32[2,128,16,128]{1,3,2,0:T(8,128)S(1)}) fusion(bf16[8,2,16,128,64]{3,4,2,1,0:T(8,128)(2,1)} %get-tuple-element.165, s32[]{:T(128)} %get-tuple-element.152, bf16[8,2,128,64]{2,3,1,0:T(8,128)(2,1)S(1)} %get-tuple-element.164, s32[2,128]{1,0:T(2,128)S(1)} %iota_add_fusion.4, ...), kind=kOutput, calls=%fused_computation.49.clone.1 | convolution fusion | flops 69730048 | bytes 2674176 | tf_op jit(solution)/shard_map/while/body/eval_jaxpr/abd,asjd->absj/dot_general | solution.py:24
  119.7 2.9 %fusion.31 = (f32[2,128]{1,0:T(2,128)S(1)}, f32[2,128,16,128]{1,3,2,0:T(8,128)S(1)}) fusion(bf16[8,2,16,128,64]{3,4,2,1,0:T(8,128)(2,1)} %get-tuple-element.165, s32[]{:T(128)} %get-tuple-element.152, bf16[8,2,128,64]{2,3,1,0:T(8,128)(2,1)S(1)} %get-tuple-element.164, s32[2,128]{1,0:T(2,128)S(1)} %iota_add_fusion.4, ...), kind=kOutput, calls=%fused_computation.49.clone.1 | convolution fusion | flops 69730048 | bytes 2674176 | tf_op jit(solution)/shard_map/while/body/eval_jaxpr/abd,asjd->absj/dot_general | solution.py:24
  125.7 2.9 %fusion.31 = (f32[2,128]{1,0:T(2,128)S(1)}, f32[2,128,16,128]{1,3,2,0:T(8,128)S(1)}) fusion(bf16[8,2,16,128,64]{3,4,2,1,0:T(8,128)(2,1)} %get-tuple-element.165, s32[]{:T(128)} %get-tuple-element.152, bf16[8,2,128,64]{2,3,1,0:T(8,128)(2,1)S(1)} %get-tuple-element.164, s32[2,128]{1,0:T(2,128)S(1)} %iota_add_fusion.4, ...), kind=kOutput, calls=%fused_computation.49.clone.1 | convolution fusion | flops 69730048 | bytes 2674176 | tf_op jit(solution)/shard_map/while/body/eval_jaxpr/abd,asjd->absj/dot_general | solution.py:24
  129.3 2.1 %fusion.33 = bf16[1,2,128,64]{2,3,1,0:T(8,128)(2,1)S(1)} fusion(f32[2,128,16,128]{1,3,2,0:T(8,128)S(1)} %get-tuple-element.142, f32[2,128]{1,0:T(2,128)S(1)} %get-tuple-element.143, s32[2,128]{1,0:T(2,128)S(1)} %iota_add_fusion.4, s32[2,16,128]{2,1,0:T(8,128)S(1)} %iota_add_fusion.5, pred[2,16]{1,0:T(4,128)(4,1)S(1)} %compare_bitcast_fusion.2, ...), kind=kOutput, calls=%fused_computation.10.clone.1 | convolution fusion | flops 69763072 | bytes 2674208 | tf_op jit(solution)/shard_map/while/body/eval_jaxpr/absj,asjd->abd/dot_general | solution.py:38
  132.3 14.6 %all_to_all.61 = bf16[8,64,256]{2,1,0:T(8,128)(2,1)S(1)} all-to-all(bf16[8,64,256]{2,1,0:T(8,128)(2,1)S(1)} %reshape.153), channel_id=1, replica_groups=mesh['uly'=8,'blk'=4] {'uly'}, dimensions={0} | all-to-all | bytes 524288 | tf_op jit(solution)/shard_map/all_to_all | solution.py:78
  (95 shorter events, 29.1 us)
Async XLA Ops:
  6.5 36.1 %copy-start = (bf16[64,2048]{1,0:T(8,128)(2,1)S(1)}, bf16[64,2048]{1,0:T(8,128)(2,1)}, u32[]{:S(2)}) copy-start(bf16[64,2048]{1,0:T(8,128)(2,1)} %param.8) | copy-start | bytes 786436
  6.5 40.4 %copy-start.1 = (s32[4,4,16]{2,1,0:T(4,128)S(1)}, s32[4,4,16]{2,1,0:T(4,128)}, u32[]{:S(2)}) copy-start(s32[4,4,16]{2,1,0:T(4,128)} %param.11) | copy-start | bytes 3076
  6.5 49.6 %all-gather.5.cloned.1.call-start = ((), (), s32[]{:S(2)}) async-start(), calls=%async_computation.5 | async-start | bytes 1310720 | tf_op jit(solution)/shard_map/all_gather | solution.py:57
  29.5 34.1 %all-gather.3.cloned.1.call-start = ((), (), s32[]{:S(2)}) async-start(), calls=%async_computation.4 | async-start | bytes 1310720 | tf_op jit(solution)/shard_map/all_gather | solution.py:56
  43.4 12.1 %all-to-all-start = ((bf16[64,8,256]{2,0,1:T(8,128)(2,1)}), bf16[64,8,256]{2,0,1:T(8,128)(2,1)S(1)}, u32[]{:S(2)}, u32[]{:S(2)}) async-start(bf16[64,8,256]{2,0,1:T(8,128)(2,1)} %bitcast.90), calls=%async_computation | async-start | bytes 524288 | tf_op jit(solution)/shard_map/all_to_all | solution.py:49
Sparse Core Ops, SparseCore 0:
  29.7 15.6 all-gather.4
  47.0 16.6 all-gather.2
